TPU v7x, 32 devices: a whole 2x2x4 slice. The times are simulated.
32 devices in a mesh: col: 4 (over y, x), row: 8 (over z, core).
Axes of the slice: x: 2, y: 2, z: 4, core: 2. Of those that a mesh axis runs over, the one named last changes fastest.
Arguments:
- velocity: bfloat16 [4, 524288], P(None, ('col', 'row')), may hold values from -6 to 6
- pair_struct: int32 [4096], P(('col', 'row')), may hold values from 0 to 63
- pair_panel: int32 [4096], P(('col', 'row')), may hold values from 0 to 127
- pair_count: int32 [32], P(('col', 'row')), may hold values from 32 to 128, as said below
- mortar_coef: bfloat16 [4096, 128, 128], P(('col', 'row')), may hold values from -0.0625 to 0.0625
- bem_matrix: bfloat16 [32768, 32768], P('row', 'col'), may hold values from -0.03125 to 0.03125
- self_term: float32 [32768], P('row'), may hold values from 0.5 to 2
Outputs:
- pressure: bfloat16 [4, 32768], P(None, 'row')
- load: float32 [4, 524288], P(None, ('col', 'row'))
Inputs may be any that keep to these rules, and one draw needn't show every extreme that they name: pair_struct numbers a structural block within the slot's own device. `pair_count`: some device has all its slots live.
All inputs are finite; a program needn't handle non-finite values.
Results may differ from a plain program's by a relative error of at most 0.005.
Values may be sent and summed in bfloat16 or wider, within the bound.
No kernel may reach another device: no remote copies, remote signals or barrier semaphores. Data moves between devices by JAX's collectives and lax.ppermute only.
A program may use at most 128 MiB of HBM per device.

v0:
```python
import jax
import jax.numpy as jnp
from jax import lax
from jax.sharding import PartitionSpec as P

PANELS = 16384


def split_parts(blocks):
    return jnp.stack([blocks[..., 0::2], blocks[..., 1::2]], axis=1)


def on_device(velocity, pair_struct, pair_panel, pair_count, mortar_coef, bem_matrix, self_term):
    cases = velocity.shape[0]
    slots = pair_struct.shape[0]
    block = mortar_coef.shape[1]
    node_blocks = velocity.shape[1] // (2 * block)
    panel_blocks = PANELS // block
    live_mask = jnp.arange(slots, dtype=jnp.int32) < pair_count[0]
    vel_blocks = velocity.reshape(cases, node_blocks, 2 * block)
    picked = split_parts(jnp.take(vel_blocks, pair_struct, axis=1))
    pair_terms = jnp.einsum(
        "qpn,ckqn->ckqp", mortar_coef, picked, preferred_element_type=jnp.float32
    )
    panel_onehot = (
        (pair_panel[:, None] == jnp.arange(panel_blocks, dtype=jnp.int32)[None, :])
        & live_mask[:, None]
    ).astype(jnp.float32)
    spread_parts = jnp.einsum(
        "qb,ckqp->ckbp", panel_onehot, pair_terms, precision=lax.Precision.HIGHEST
    )
    spread_sum = spread_parts.transpose(0, 2, 3, 1).reshape(cases, 2 * PANELS)
    width_col = 2 * PANELS // lax.axis_size("col")
    width_row = 2 * PANELS // lax.axis_size("row")
    whole_sum = lax.psum(spread_sum, ("col", "row"))
    columns = lax.dynamic_slice_in_dim(
        whole_sum, lax.axis_index("col") * width_col, width_col, 1
    ).astype(jnp.bfloat16)
    row_start = lax.axis_index("row") * width_row
    owner = row_start // width_col == lax.axis_index("col")
    own_part = lax.dynamic_slice_in_dim(columns, row_start % width_col, width_row, 1).astype(
        jnp.float32
    )
    partial_value = lax.dot_general(
        columns, bem_matrix, (((1,), (1,)), ((), ())), preferred_element_type=jnp.float32
    )
    partial_value = partial_value + jnp.where(owner, self_term[None, :] * own_part, 0.0)
    pressure = lax.psum(partial_value, "col").astype(jnp.bfloat16)
    full_pressure = lax.all_gather(pressure, "row", axis=1, tiled=True)
    panel_view = full_pressure.reshape(cases, panel_blocks, 2 * block)
    took = split_parts(jnp.take(panel_view, pair_panel, axis=1))
    back_terms = jnp.einsum("qpn,ckqp->ckqn", mortar_coef, took, preferred_element_type=jnp.float32)
    node_onehot = (
        (pair_struct[:, None] == jnp.arange(node_blocks, dtype=jnp.int32)[None, :])
        & live_mask[:, None]
    ).astype(jnp.float32)
    load_parts = jnp.einsum(
        "qs,ckqn->cksn", node_onehot, back_terms, precision=lax.Precision.HIGHEST
    )
    load = load_parts.transpose(0, 2, 3, 1).reshape(cases, 2 * node_blocks * block)
    return (pressure, load)


def solution(mesh):
    placed = (
        P(None, ("col", "row")),
        P(("col", "row")),
        P(("col", "row")),
        P(("col", "row")),
        P(("col", "row"), None, None),
        P("row", "col"),
        P("row"),
    )
    return jax.shard_map(
        on_device,
        mesh=mesh,
        in_specs=placed,
        out_specs=(P(None, "row"), P(None, ("col", "row"))),
        check_vma=False,
    )
```

profile of v0, /device:TPU:0, one launch (start us, length us, event | category | flops | bytes accessed | tf_op | source)
XLA Modules:
  0.0 174.2 jit_solution(17576854343563618886)
XLA Ops:
  0.7 0.9 copy-done
  1.5 0.7 compare_select_fusion.1
  2.2 0.8 gather_fusion
  3.0 0.7 compare_and_fusion.1
  3.7 0.2 select_bitcast_fusion.1
  3.9 5.7 %slice.13 = bf16[4,128,128]{2,0,1:T(4,128)(2,1)S(1)} slice(bf16[4,128,256]{2,0,1:T(4,128)(2,1)S(1)} %select_bitcast_fusion.1), slice={[0:4:1], [0:128:1], [1:256:2]} | slice | bytes 262144 | tf_op jit(solution)/shard_map/slice | solution.py:10
  9.7 5.7 %slice.12 = bf16[4,128,128]{2,0,1:T(4,128)(2,1)S(1)} slice(bf16[4,128,256]{2,0,1:T(4,128)(2,1)S(1)} %select_bitcast_fusion.1), slice={[0:4:1], [0:128:1], [0:256:2]} | slice | bytes 262144 | tf_op jit(solution)/shard_map/slice | solution.py:10
  15.4 4.4 %fusion.2 = f32[128,4,2,128]{3,1,2,0:T(4,128)S(1)} fusion(bf16[128,128,128]{2,1,0:T(8,128)(2,1)} %param.11, bf16[4,1,128,128]{3,0,2,1:T(4,128)(2,1)S(1)} %bitcast.47, bf16[4,1,128,128]{3,0,2,1:T(4,128)(2,1)S(1)} %bitcast.48), kind=kOutput, calls=%fused_computation.5 | convolution fusion | flops 33685504 | bytes 4980736 | tf_op jit(solution)/shard_map/qpn,ckqn->ckqp/dot_general | solution.py:22
  19.8 0.3 copy.16
  20.8 0.5 convolution_bitcast_fusion
  21.2 12.1 %copy.9 = f32[4,128,128,2]{0,3,2,1:T(2,128)} copy(f32[4,128,128,2]{1,2,3,0:T(8,128)S(1)} %convolution_bitcast_fusion) | data formatting | bytes 1048576 | tf_op jit(solution)/shard_map/transpose;qb,ckqp->ckbp/transpose | solution.py:32
  33.4 9.5 %copy.10 = f32[4,32768]{1,0:T(4,128)S(1)} copy(f32[4,32768]{0,1:T(8,128)} %bitcast.44) | data formatting | bytes 1048576 | tf_op jit(solution)/shard_map/reshape | solution.py:32
  42.9 47.2 %all-reduce.1 = bf16[4,32768]{1,0:T(4,128)(2,1)S(1)} all-reduce(f32[4,32768]{1,0:T(4,128)S(1)} %copy.10), channel_id=1, replica_groups=mesh['col'=4,'row'=8] {'col','row'}, use_global_device_ids=true, to_apply=%region_0.1 | all-reduce | flops 131072 | bytes 786432 | tf_op jit(solution)/shard_map/psum | solution.py:35
  90.2 25.4 %convolution_add_fusion = f32[4,4096]{1,0:T(4,128)S(1)} fusion(bf16[4,8192]{1,0:T(4,128)(2,1)S(1)} %dynamic-slice_convert_fusion, bf16[4096,8192]{1,0:T(8,128)(2,1)} %param.12, s32[]{:T(128)S(6)} %select_n.48, f32[4096]{0:T(1024)S(1)} %copy-done.2, pred[]{:T(512)S(6)} %eq.34), kind=kOutput, calls=%fused_computation.2 | convolution fusion | flops 268500992 | bytes 67289096 | tf_op jit(solution)/shard_map/dot_general | solution.py:44
  115.6 16.1 %psum.15 = bf16[4,4096]{1,0:T(4,128)(2,1)S(1)} all-reduce(f32[4,4096]{1,0:T(4,128)S(1)} %convolution_add_fusion), channel_id=1, replica_groups=mesh['col'=4,'row'=8] {'col'}, use_global_device_ids=true, to_apply=%region_1.2 | all-reduce | flops 16384 | bytes 98304 | tf_op jit(solution)/shard_map/psum | solution.py:48
  131.7 14.4 %all_gather.3 = bf16[4,32768]{1,0:T(4,128)(2,1)S(1)} all-gather(bf16[4,4096]{1,0:T(4,128)(2,1)S(1)} %psum.15), channel_id=1, replica_groups=mesh['col'=4,'row'=8] {'row'}, dimensions={1}, use_global_device_ids=true | all-gather | bytes 294912 | tf_op jit(solution)/shard_map/all_gather | solution.py:49
  146.1 0.8 gather_fusion.1
  146.9 0.2 select_bitcast_fusion
  147.2 5.7 %slice.15 = bf16[4,128,128]{2,0,1:T(4,128)(2,1)S(1)} slice(bf16[4,128,256]{2,0,1:T(4,128)(2,1)S(1)} %select_bitcast_fusion), slice={[0:4:1], [0:128:1], [1:256:2]} | slice | bytes 262144 | tf_op jit(solution)/shard_map/slice | solution.py:10
  152.9 5.7 %slice.14 = bf16[4,128,128]{2,0,1:T(4,128)(2,1)S(1)} slice(bf16[4,128,256]{2,0,1:T(4,128)(2,1)S(1)} %select_bitcast_fusion), slice={[0:4:1], [0:128:1], [0:256:2]} | slice | bytes 262144 | tf_op jit(solution)/shard_map/slice | solution.py:10
  158.6 3.4 %fusion = f32[128,4,2,128]{3,1,2,0:T(4,128)S(1)} fusion(bf16[128,128,128]{2,1,0:T(8,128)(2,1)} %param.11, bf16[4,1,128,128]{3,0,2,1:T(4,128)(2,1)S(1)} %bitcast.49, bf16[4,1,128,128]{3,0,2,1:T(4,128)(2,1)S(1)} %bitcast.50), kind=kOutput, calls=%fused_computation.3 | convolution fusion | flops 33685504 | bytes 4980736 | tf_op jit(solution)/shard_map/qpn,ckqp->ckqn/dot_general | solution.py:52
  162.0 0.4 convolution_bitcast_fusion.1
  162.4 5.9 %copy.12 = f32[4,64,128,2]{0,3,2,1:T(2,128)} copy(f32[4,64,128,2]{2,1,3,0:T(8,128)S(1)} %convolution_bitcast_fusion.1) | data formatting | bytes 524288 | tf_op jit(solution)/shard_map/transpose;qs,ckqn->cksn/transpose | solution.py:60
  168.3 5.9 %copy.13 = f32[4,16384]{1,0:T(4,128)} copy(f32[4,16384]{0,1:T(8,128)} %bitcast.45) | data formatting | bytes 524288
  (15 shorter events, 0.1 us)
Async XLA Ops:
  0.6 0.9 copy-start
  0.6 20.1 %copy-start.3 = (s32[128]{0:T(128)S(1)}, s32[128]{0:T(128)}, u32[]{:S(2)}) copy-start(s32[128]{0:T(128)} %param.9) | copy-start | bytes 1540
  33.4 56.8 %copy-start.2 = (f32[4096]{0:T(1024)S(1)}, f32[4096]{0:T(1024)}, u32[]{:S(2)}) copy-start(f32[4096]{0:T(1024)} %param.13) | copy-start | bytes 49156
  115.6 46.4 %copy-start.4 = (s32[128]{0:T(128)S(1)}, s32[128]{0:T(128)}, u32[]{:S(2)}) copy-start(s32[128]{0:T(128)} %param.8) | copy-start | bytes 1540
  131.7 36.6 %copy-start.1 = (bf16[4,4096]{1,0:T(4,128)(2,1)}, bf16[4,4096]{1,0:T(4,128)(2,1)S(1)}, u32[]{:S(2)}) copy-start(bf16[4,4096]{1,0:T(4,128)(2,1)S(1)} %psum.15) | copy-start | bytes 98308
where the time goes:
time: 175 us; the launch traced here: 174 us
  blocking collectives  77.7 us (44%)
  local copies, waits for them, and re-layouts  59.1 us (34%)
  matrix products  34.1 us (19%)
  other arithmetic  1.8 us (1%)
    psum x1, blocking collectives, on_device(): whole_sum = lax.psum(spread_sum, ('col', 'row'))  47.2 us
    dot_general x1, matrix products, on_device(): lax.dot_general(columns, bem_matrix, (((1,), (1,)), ((), ())), preferred_...  25.4 us
    slice x4, local copies, waits for them, and re-layouts, split_parts(): return jnp.stack([blocks[..., 0::2], blocks[..., 1::2]], axis=1)  22.9 us
    psum x1, blocking collectives, on_device(): pressure = lax.psum(partial_value, 'col').astype(jnp.bfloat16)  16.1 us
    all_gather x1, blocking collectives, on_device(): full_pressure = lax.all_gather(pressure, 'row', axis=1, tiled=True)  14.4 us
    transpose x1, local copies, waits for them, and re-layouts, on_device(): spread_sum = spread_parts.transpose(0, 2, 3, 1).reshape(cases, 2 * PANELS)  12.1 us
    reshape x1, local copies, waits for them, and re-layouts, on_device(): spread_sum = spread_parts.transpose(0, 2, 3, 1).reshape(cases, 2 * PANELS)  9.48 us
    unnamed x11, local copies, waits for them, and re-layouts  6.83 us

commit v1 on v0

--- a/solution.py
+++ b/solution.py
@@ -32,7 +32,7 @@
     spread_sum = spread_parts.transpose(0, 2, 3, 1).reshape(cases, 2 * PANELS)
     width_col = 2 * PANELS // lax.axis_size("col")
     width_row = 2 * PANELS // lax.axis_size("row")
-    whole_sum = lax.psum(spread_sum, ("col", "row"))
+    whole_sum = jnp.sum(lax.all_gather(spread_sum, ("col", "row")), axis=0)
     columns = lax.dynamic_slice_in_dim(
         whole_sum, lax.axis_index("col") * width_col, width_col, 1
     ).astype(jnp.bfloat16)

time: 175 us -> 267 us (1.53)
  waiting for transfers between devices: 0 us -> 117 us
  blocking collectives: 77.7 us -> 30.3 us
  between operations: 1.5 us -> 14.9 us
  other arithmetic: 1.8 us -> 10.6 us
    all_gather x0 -> x1, waiting for transfers between devices: none -> 117 us  [on_device(): whole_sum = jnp.sum(lax.all_gather(spread_sum, ('col', 'row')), axis=0)]
    psum x1 -> x0, blocking collectives: 47.2 us -> none  [on_device(): whole_sum = lax.psum(spread_sum, ('col', 'row'))]
    another operation x0 -> x1, local copies, waits for them, and re-layouts: none -> 9.83 us  [on_device(): whole_sum = jnp.sum(lax.all_gather(spread_sum, ('col', 'row')), axis=0)]
    reshape x1 -> x0, local copies, waits for them, and re-layouts: 9.48 us -> none  [on_device(): spread_sum = spread_parts.transpose(0, 2, 3, 1).reshape(cases, 2 * PANELS)]
    reduce_sum x0 -> x1, other arithmetic: none -> 8.79 us  [on_device(): whole_sum = jnp.sum(lax.all_gather(spread_sum, ('col', 'row')), axis=0)]
  transfers between devices with their start and end apart: 0 -> 1, of which waited for: 0 -> 1; matrix products, arithmetic and copies ran while one was open for 0% -> 0% of each run, Pallas kernels for 0% -> 0%
where the time goes in v1:
time: 267 us; the launch traced here: 266 us
  waiting for transfers between devices  117 us (44%)
  local copies, waits for them, and re-layouts  58.3 us (22%)
  matrix products  35 us (13%)
  blocking collectives  30.3 us (11%)
  between operations  14.9 us (6%)
  other arithmetic  10.6 us (4%)
    all_gather x1, waiting for transfers between devices, on_device(): whole_sum = jnp.sum(lax.all_gather(spread_sum, ('col', 'row')), axis=0)  117 us
    dot_general x1, matrix products, on_device(): lax.dot_general(columns, bem_matrix, (((1,), (1,)), ((), ())), preferred_...  25.4 us
    slice x4, local copies, waits for them, and re-layouts, split_parts(): return jnp.stack([blocks[..., 0::2], blocks[..., 1::2]], axis=1)  22.9 us
    psum x1, blocking collectives, on_device(): pressure = lax.psum(partial_value, 'col').astype(jnp.bfloat16)  15.9 us
    all_gather x1, blocking collectives, on_device(): full_pressure = lax.all_gather(pressure, 'row', axis=1, tiled=True)  14.4 us
    transpose x1, local copies, waits for them, and re-layouts, on_device(): spread_sum = spread_parts.transpose(0, 2, 3, 1).reshape(cases, 2 * PANELS)  12.1 us
    another operation x1, local copies, waits for them, and re-layouts, on_device(): whole_sum = jnp.sum(lax.all_gather(spread_sum, ('col', 'row')), axis=0)  9.83 us
    reduce_sum x1, other arithmetic, on_device(): whole_sum = jnp.sum(lax.all_gather(spread_sum, ('col', 'row')), axis=0)  8.79 us
  transfers between devices with their start and end apart: 1, of which 1 were waited for; matrix products, arithmetic and copies ran while one was open for 0% of the time, Pallas kernels for 0%

profile of v1, /device:TPU:0, one launch (start us, length us, event | category | flops | bytes accessed | tf_op | source)
XLA Modules:
  0.0 266.3 jit_solution(2475848525754027526)
XLA Ops:
  7.2 0.0 all-gather.2.cloned.1.call-start
  7.2 0.7 compare_select_fusion.1
  7.9 0.7 compare_and_fusion.1
  8.6 0.8 gather_fusion
  9.4 0.2 select_bitcast_fusion.1
  9.7 5.7 %slice.13 = bf16[4,128,128]{2,0,1:T(4,128)(2,1)S(1)} slice(bf16[4,128,256]{2,0,1:T(4,128)(2,1)S(1)} %select_bitcast_fusion.1), slice={[0:4:1], [0:128:1], [1:256:2]} | slice | bytes 262144 | tf_op jit(solution)/shard_map/slice | solution.py:10
  15.4 5.7 %slice.12 = bf16[4,128,128]{2,0,1:T(4,128)(2,1)S(1)} slice(bf16[4,128,256]{2,0,1:T(4,128)(2,1)S(1)} %select_bitcast_fusion.1), slice={[0:4:1], [0:128:1], [0:256:2]} | slice | bytes 262144 | tf_op jit(solution)/shard_map/slice | solution.py:10
  21.8 4.4 %fusion.4 = f32[4,2,128,128]{3,0,1,2:T(4,128)S(1)} fusion(bf16[128,128,128]{2,1,0:T(8,128)(2,1)} %param.11, bf16[4,1,128,128]{3,0,1,2:T(4,128)(2,1)S(1)} %bitcast.51, bf16[4,1,128,128]{3,0,1,2:T(4,128)(2,1)S(1)} %bitcast.52), kind=kOutput, calls=%fused_computation.7 | convolution fusion | flops 34078720 | bytes 4980736 | tf_op jit(solution)/shard_map/qpn,ckqn->ckqp/dot_general | solution.py:22
  26.2 1.3 convolution_bitcast_fusion
  27.6 12.1 %copy.15 = f32[4,128,128,2]{0,3,2,1:T(2,128)} copy(f32[4,128,128,2]{1,2,3,0:T(8,128)S(1)} %convolution_bitcast_fusion) | data formatting | bytes 1048576 | tf_op jit(solution)/shard_map/transpose;qb,ckqp->ckbp/transpose | solution.py:32
  39.7 9.8 %copy.16 = f32[1,4,32768]{2,1,0:T(4,128)} copy(f32[1,4,32768]{1,2,0:T(8,128)} %bitcast.48) | data formatting | bytes 1048576 | tf_op jit(solution)/shard_map/all_gather;reshape | solution.py:35
  49.6 117.2 %all-gather.2.cloned.1.call-done = f32[32,4,32768]{2,1,0:T(4,128)} async-done(((f32[1,4,32768]{2,1,0:T(4,128)}), f32[32,4,32768]{2,1,0:T(4,128)}) %all-gather.2.cloned.1.call-update) | async-done | bytes 16777232 | tf_op jit(solution)/shard_map/all_gather | solution.py:35
  166.8 8.8 %reduce_sum.9 = bf16[4,32768]{1,0:T(4,128)(2,1)S(1)} reduce(f32[32,4,32768]{2,1,0:T(4,128)} %all-gather.2.cloned.1.call-done, f32[]{:T(128)} %constant.58.clone.1), dimensions={0}, to_apply=%region_0.1 | reduce | flops 4063232 | bytes 17039364 | tf_op jit(solution)/shard_map/reduce_sum | solution.py:35
  175.6 25.4 %convolution_add_fusion = f32[4,4096]{1,0:T(4,128)S(1)} fusion(bf16[4,8192]{1,0:T(4,128)(2,1)S(1)} %dynamic-slice_convert_fusion, bf16[4096,8192]{1,0:T(8,128)(2,1)} %param.12, s32[]{:T(128)S(6)} %select_n.48, f32[4096]{0:T(1024)S(1)} %copy-done.2, pred[]{:T(512)S(6)} %eq.34), kind=kOutput, calls=%fused_computation.2 | convolution fusion | flops 268500992 | bytes 67289096 | tf_op jit(solution)/shard_map/dot_general | solution.py:44
  201.0 15.9 %psum.7 = bf16[4,4096]{1,0:T(4,128)(2,1)S(1)} all-reduce(f32[4,4096]{1,0:T(4,128)S(1)} %convolution_add_fusion), channel_id=1, replica_groups=mesh['col'=4,'row'=8] {'col'}, use_global_device_ids=true, to_apply=%region_1.2 | all-reduce | flops 16384 | bytes 98304 | tf_op jit(solution)/shard_map/psum | solution.py:48
  217.0 14.4 %all_gather.7 = bf16[4,32768]{1,0:T(4,128)(2,1)S(1)} all-gather(bf16[4,4096]{1,0:T(4,128)(2,1)S(1)} %psum.7), channel_id=1, replica_groups=mesh['col'=4,'row'=8] {'row'}, dimensions={1}, use_global_device_ids=true | all-gather | bytes 294912 | tf_op jit(solution)/shard_map/all_gather | solution.py:49
  231.4 0.8 gather_fusion.1
  232.2 0.2 select_bitcast_fusion
  232.4 5.7 %slice.15 = bf16[4,128,128]{2,0,1:T(4,128)(2,1)S(1)} slice(bf16[4,128,256]{2,0,1:T(4,128)(2,1)S(1)} %select_bitcast_fusion), slice={[0:4:1], [0:128:1], [1:256:2]} | slice | bytes 262144 | tf_op jit(solution)/shard_map/slice | solution.py:10
  238.2 5.7 %slice.14 = bf16[4,128,128]{2,0,1:T(4,128)(2,1)S(1)} slice(bf16[4,128,256]{2,0,1:T(4,128)(2,1)S(1)} %select_bitcast_fusion), slice={[0:4:1], [0:128:1], [0:256:2]} | slice | bytes 262144 | tf_op jit(solution)/shard_map/slice | solution.py:10
  243.9 3.4 %fusion.7 = f32[4,2,128,128]{3,0,1,2:T(4,128)S(1)} fusion(bf16[128,128,128]{2,1,0:T(8,128)(2,1)} %param.11, bf16[4,1,128,128]{3,0,2,1:T(4,128)(2,1)S(1)} %bitcast.53, bf16[4,1,128,128]{3,0,2,1:T(4,128)(2,1)S(1)} %bitcast.54), kind=kOutput, calls=%fused_computation.8 | convolution fusion | flops 33685504 | bytes 4980736 | tf_op jit(solution)/shard_map/qpn,ckqp->ckqn/dot_general | solution.py:52
  247.3 0.4 convolution_bitcast_fusion.1
  247.7 5.9 %copy.22 = f32[4,64,128,2]{0,3,2,1:T(2,128)} copy(f32[4,64,128,2]{2,1,3,0:T(8,128)S(1)} %convolution_bitcast_fusion.1) | data formatting | bytes 524288 | tf_op jit(solution)/shard_map/transpose;qs,ckqn->cksn/transpose | solution.py:60
  253.6 5.9 %copy.23 = f32[4,16384]{1,0:T(4,128)} copy(f32[4,16384]{0,1:T(8,128)} %bitcast.49) | data formatting | bytes 524288
  (17 shorter events, 0.1 us)
Async XLA Ops:
  7.2 1.4 copy-start
  7.2 159.6 %all-gather.2.cloned.1.call-start = ((), (), s32[]{:S(2)}) async-start(), calls=%async_computation | async-start | bytes 17301504 | tf_op jit(solution)/shard_map/all_gather | solution.py:35
  39.6 9.9 %copy-start.3 = (s32[128]{0:T(128)S(1)}, s32[128]{0:T(128)}, u32[]{:S(2)}) copy-start(s32[128]{0:T(128)} %param.9) | copy-start | bytes 1540
  49.6 126.0 %copy-start.2 = (f32[4096]{0:T(1024)S(1)}, f32[4096]{0:T(1024)}, u32[]{:S(2)}) copy-start(f32[4096]{0:T(1024)} %param.13) | copy-start | bytes 49156
  175.6 71.7 %copy-start.4 = (s32[128]{0:T(128)S(1)}, s32[128]{0:T(128)}, u32[]{:S(2)}) copy-start(s32[128]{0:T(128)} %param.8) | copy-start | bytes 1540
  217.0 42.5 %copy-start.1 = (bf16[4,4096]{1,0:T(4,128)(2,1)}, bf16[4,4096]{1,0:T(4,128)(2,1)S(1)}, u32[]{:S(2)}) copy-start(bf16[4,4096]{1,0:T(4,128)(2,1)S(1)} %psum.7) | copy-start | bytes 98308
Sparse Core Ops, SparseCore 0:
  49.6 117.0 all-gather.1
